TPU v7x, 32 devices: a whole 2x2x4 slice. The times are simulated.
32 devices in a mesh: row: 8 (over y, x, core), col: 4 (over z).
Axes of the slice: x: 2, y: 2, z: 4, core: 2. Of those that a mesh axis runs over, the one named last changes fastest.
Arguments:
- tensor: float32 [128, 128, 768], P('row', 'col'), may hold values from -6 to 6
- start_one: float32 [128, 64], P('row'), may hold values from -0.5 to 0.5
- start_two: float32 [128, 64], P('col'), may hold values from -0.5 to 0.5
- start_three: float32 [768, 64], replicated, may hold values from -0.21875 to 0.21875
Outputs:
- factor_one: float32 [128, 64], replicated
- factor_two: float32 [128, 64], replicated
- factor_three: float32 [768, 64], replicated
- core: float32 [64, 64, 64], P(None, 'row', 'col')
All inputs are finite; a program needn't handle non-finite values.
Results may differ from a plain program's by a relative error of at most 0.0003.
Values sent between devices are 32-bit elements; how exact they have to be, the bound alone decides.
A program may use at most 64 MiB of HBM per device.

v0:
```python
import math
import jax
import jax.numpy as jnp
from jax import lax
from jax.sharding import PartitionSpec as P

STEPS = 4
HIGHEST = lax.Precision.HIGHEST


def product(left, right):
    return jnp.dot(left, right, precision=HIGHEST, preferred_element_type=jnp.float32)


def left_product(left, right):
    return lax.dot_general(
        left, right, (((0,), (0,)), ((), ())), precision=HIGHEST, preferred_element_type=jnp.float32
    )


def right_product(left, right):
    return lax.dot_general(
        left, right, (((1,), (1,)), ((), ())), precision=HIGHEST, preferred_element_type=jnp.float32
    )


def cross_product(left, right):
    return lax.dot_general(
        left, right, (((0,), (1,)), ((), ())), precision=HIGHEST, preferred_element_type=jnp.float32
    )


def orthonormal(matrix, inner):
    lower = jnp.linalg.cholesky(inner)
    return jax.scipy.linalg.solve_triangular(lower, matrix.T, lower=True).T


def pairing(local, block_rows):
    return right_product(local, block_rows)


def settle(gram_whole, basis):
    for iteration in range(STEPS):
        image = product(gram_whole, basis)
        basis = orthonormal(image, left_product(image, image))
    return basis


def on_device(tensor, start_one, start_two, start_three):
    rows_one, rows_two, depth = tensor.shape
    rank = start_three.shape[1]
    flat = tensor.reshape(rows_one * rows_two, depth)
    contracted = cross_product(start_three, flat).reshape(rank, rows_one, rows_two)
    part_one = jnp.einsum("cij,jb->ibc", contracted, start_two, precision=HIGHEST).reshape(
        rows_one, rank * rank
    )
    slab_one = lax.psum_scatter(part_one, "col", scatter_dimension=1, tiled=True)
    slab_rows_one = lax.all_gather(slab_one, "row", axis=0, tiled=True)
    gram_one = lax.psum(right_product(slab_rows_one, slab_rows_one), "col")
    basis_one = settle(gram_one, lax.all_gather(start_one, "row", axis=0, tiled=True))
    own_one = lax.dynamic_slice_in_dim(basis_one, lax.axis_index("row") * rows_one, rows_one, 0)
    part_two = jnp.einsum("cij,ia->jac", contracted, own_one, precision=HIGHEST).reshape(
        rows_two, rank * rank
    )
    slab_two = lax.psum_scatter(part_two, "row", scatter_dimension=1, tiled=True)
    slab_rows_two = lax.all_gather(slab_two, "col", axis=0, tiled=True)
    gram_two = lax.psum(right_product(slab_rows_two, slab_rows_two), "row")
    basis_two = settle(gram_two, lax.all_gather(start_two, "col", axis=0, tiled=True))
    own_two = lax.dynamic_slice_in_dim(basis_two, lax.axis_index("col") * rows_two, rows_two, 0)
    received = lax.all_to_all(tensor, "row", split_axis=2, concat_axis=0, tiled=True)
    count, items, cells = received.shape
    merged = left_product(basis_one, received.reshape(count, items * cells))
    mixed = merged.reshape(rank, items, cells)
    part_three = jnp.einsum("ajk,jb->kba", mixed, own_two, precision=HIGHEST)
    cells_here = part_three.shape[0]
    slab_three = lax.psum_scatter(
        part_three.reshape(cells_here, rank * rank), "col", scatter_dimension=1, tiled=True
    )
    gram_part_three = pairing(slab_three, lax.all_gather(slab_three, "row", axis=0, tiled=True))
    gram_three = lax.psum(gram_part_three, "col")
    basis_three = start_three
    own_three = start_three
    for iteration in range(STEPS):
        image = product(gram_three, basis_three)
        inner = lax.psum(left_product(image, image), "row")
        own_three = orthonormal(image, inner)
        basis_three = lax.all_gather(own_three, "row", axis=0, tiled=True)
    core_part = left_product(own_three, slab_three)
    core_part = core_part.reshape(rank, core_part.shape[1] // rank, rank)
    core = lax.psum_scatter(core_part, "row", scatter_dimension=2, tiled=True).transpose(0, 2, 1)
    factor_one = basis_one * math.sqrt(basis_one.shape[0])
    factor_two = basis_two * math.sqrt(basis_two.shape[0])
    factor_three = basis_three * math.sqrt(basis_three.shape[0])
    return (factor_one, factor_two, factor_three, core)


def solution(mesh):
    return jax.shard_map(
        on_device,
        mesh=mesh,
        in_specs=(P("row", "col", None), P("row", None), P("col", None), P()),
        out_specs=(P(), P(), P(), P(None, "row", "col")),
        check_vma=False,
    )
```

profile of v0, /device:TPU:0, one launch (start us, length us, event | category | flops | bytes accessed | tf_op | source)
XLA Modules:
  0.0 638.1 jit_solution(973068163309146630)
XLA Ops:
  8.1 2.8 fusion.2
  13.1 22.8 %reduce-scatter.5.cloned.1.call-done = f32[16,1024]{1,0:T(8,128)} async-done(((f32[16,4096]{1,0:T(8,128)}), f32[16,1024]{1,0:T(8,128)}) %reduce-scatter.5.cloned.1.call-update) | async-done | bytes 65552 | tf_op jit(solution)/shard_map/reduce_scatter | solution.py:57
  35.9 10.1 %all_gather.27 = f32[128,1024]{1,0:T(8,128)S(1)} all-gather(f32[16,1024]{1,0:T(8,128)} %reduce-scatter.5.cloned.1.call-done), channel_id=1, replica_groups=mesh['row'=8,'col'=4] {'row'}, dimensions={0}, use_global_device_ids=true | all-gather | bytes 589824 | tf_op jit(solution)/shard_map/all_gather | solution.py:58
  46.0 1.2 fusion.76
  47.2 5.0 copy.67
  52.3 7.6 %reshape.61 = f32[8,1,49152]{2,1,0:T(1,128)} reshape(f32[768,16,32]{2,1,0:T(8,128)} %bitcast.262) | data formatting | bytes 3145728
  59.9 3.7 all-to-all-start
  63.7 24.3 %all_gather.28 = f32[128,64]{1,0:T(8,128)S(1)} all-gather(f32[16,64]{1,0:T(8,128)S(1)} %copy-done.7), channel_id=1, replica_groups=mesh['row'=8,'col'=4] {'row'}, dimensions={0}, use_global_device_ids=true | all-gather | bytes 36864 | tf_op jit(solution)/shard_map/all_gather | solution.py:60
  88.0 1.2 fusion.77
  89.5 5.8 cholesky.194
  96.7 4.9 custom-call.18
  103.2 5.8 cholesky.205
  110.4 4.9 custom-call.19
  115.5 1.1 fusion.81
  116.9 5.8 cholesky.216
  124.1 4.9 custom-call.20
  129.8 5.8 cholesky.227
  137.0 4.9 custom-call.21
  143.2 1.1 reshape.42
  144.4 13.1 %all_gather.30 = f32[128,64]{1,0:T(8,128)S(1)} all-gather(f32[32,64]{1,0:T(8,128)S(1)} %copy-done.6), channel_id=1, replica_groups=mesh['row'=8,'col'=4] {'col'}, dimensions={0}, use_global_device_ids=true | all-gather | bytes 40960 | tf_op jit(solution)/shard_map/all_gather | solution.py:68
  157.6 18.4 %reduce-scatter.7.cloned.1.call-done = f32[32,512]{1,0:T(8,128)} async-done(((f32[32,4096]{1,0:T(8,128)}), f32[32,512]{1,0:T(8,128)}) %reduce-scatter.7.cloned.1.call-update) | async-done | bytes 65552 | tf_op jit(solution)/shard_map/reduce_scatter | solution.py:65
  176.0 14.0 %all_gather.29 = f32[128,512]{1,0:T(8,128)S(1)} all-gather(f32[32,512]{1,0:T(8,128)} %reduce-scatter.7.cloned.1.call-done), channel_id=1, replica_groups=mesh['row'=8,'col'=4] {'col'}, dimensions={0}, use_global_device_ids=true | all-gather | bytes 327680 | tf_op jit(solution)/shard_map/all_gather | solution.py:66
  191.8 4.4 reduce.4
  196.2 4.7 reshape.62
  200.9 5.2 copy.68
  206.2 2.3 reshape.43
  208.5 1.9 copy.69
  210.4 3.5 fusion.29
  213.9 31.0 %all-reduce.6.cloned.1.call-done = f32[128,128]{1,0:T(8,128)} async-done(((f32[128,128]{1,0:T(8,128)}), f32[128,128]{1,0:T(8,128)}) %all-reduce.6.cloned.1.call-update) | async-done | bytes 65552 | tf_op jit(solution)/shard_map/psum | solution.py:67
  245.0 1.2 fusion.86
  246.4 5.8 cholesky.238
  253.6 4.9 custom-call.22
  260.1 5.8 cholesky.249
  267.3 4.9 custom-call.23
  273.9 5.8 cholesky.260
  281.0 4.9 custom-call.24
  286.7 5.8 cholesky.271
  293.9 5.0 custom-call.25
  299.2 2.3 convolution_bitcast_fusion
  301.5 2.6 copy.72
  304.2 43.1 %reduce-scatter.9.cloned.1.call-done = f32[96,1024]{0,1:T(8,128)} async-done(((f32[96,4096]{0,1:T(8,128)}), f32[96,1024]{0,1:T(8,128)}) %reduce-scatter.9.cloned.1.call-update) | async-done | bytes 393232 | tf_op jit(solution)/shard_map/reduce_scatter | solution.py:76
  347.3 2.0 copy.73
  349.4 31.5 %all-gather.6.cloned.1.call-done = f32[768,1024]{1,0:T(8,128)} async-done(((f32[96,1024]{1,0:T(8,128)}), f32[768,1024]{1,0:T(8,128)}) %all-gather.6.cloned.1.call-update) | async-done | bytes 3145744 | tf_op jit(solution)/shard_map/all_gather | solution.py:79
  380.9 5.3 fusion.94
  386.9 35.4 %all-reduce.8.cloned.1.call-done = f32[96,768]{1,0:T(8,128)} async-done(((f32[96,768]{1,0:T(8,128)}), f32[96,768]{1,0:T(8,128)}) %all-reduce.8.cloned.1.call-update) | async-done | bytes 294928 | tf_op jit(solution)/shard_map/psum | solution.py:80
  422.3 1.5 fusion.95
  424.0 22.4 %psum.52 = f32[64,64]{0,1:T(8,128)S(1)} all-reduce(f32[64,64]{0,1:T(8,128)S(1)} %fusion.96), channel_id=1, replica_groups=mesh['row'=8,'col'=4] {'row'}, use_global_device_ids=true, to_apply=%region_8.11 | all-reduce | flops 4096 | bytes 32768 | tf_op jit(solution)/shard_map/psum | solution.py:85
  446.4 5.8 cholesky.282
  453.6 4.9 custom-call.26
  458.8 9.3 %all-gather = f32[8,96,64]{1,2,0:T(8,128)S(1)} all-gather(f32[1,96,64]{1,2,0:T(8,128)S(1)} %convolution_bitcast_fusion.5), channel_id=1, replica_groups=mesh['row'=8,'col'=4] {'row'}, dimensions={0}, use_global_device_ids=true | all-gather | bytes 221184 | tf_op jit(solution)/shard_map/all_gather | solution.py:87
  469.0 23.9 %psum.53 = f32[64,64]{0,1:T(8,128)S(1)} all-reduce(f32[64,64]{0,1:T(8,128)S(1)} %fusion.98), channel_id=1, replica_groups=mesh['row'=8,'col'=4] {'row'}, use_global_device_ids=true, to_apply=%region_9.0 | all-reduce | flops 4096 | bytes 32768 | tf_op jit(solution)/shard_map/psum | solution.py:85
  493.0 5.8 cholesky.293
  500.2 4.9 custom-call.27
  505.3 8.3 %all-gather.1 = f32[8,96,64]{1,2,0:T(8,128)S(1)} all-gather(f32[1,96,64]{1,2,0:T(8,128)S(1)} %convolution_bitcast_fusion.4), channel_id=1, replica_groups=mesh['row'=8,'col'=4] {'row'}, dimensions={0}, use_global_device_ids=true | all-gather | bytes 221184 | tf_op jit(solution)/shard_map/all_gather | solution.py:87
  514.6 23.6 %psum.54 = f32[64,64]{0,1:T(8,128)S(1)} all-reduce(f32[64,64]{0,1:T(8,128)S(1)} %fusion.100), channel_id=1, replica_groups=mesh['row'=8,'col'=4] {'row'}, use_global_device_ids=true, to_apply=%region_10.0 | all-reduce | flops 4096 | bytes 32768 | tf_op jit(solution)/shard_map/psum | solution.py:85
  538.3 5.8 cholesky.304
  545.5 4.9 custom-call.28
  550.6 9.3 %all-gather.2 = f32[8,96,64]{1,2,0:T(8,128)S(1)} all-gather(f32[1,96,64]{1,2,0:T(8,128)S(1)} %convolution_bitcast_fusion.3), channel_id=1, replica_groups=mesh['row'=8,'col'=4] {'row'}, dimensions={0}, use_global_device_ids=true | all-gather | bytes 221184 | tf_op jit(solution)/shard_map/all_gather | solution.py:87
  560.8 23.6 %psum.55 = f32[64,64]{0,1:T(8,128)S(1)} all-reduce(f32[64,64]{0,1:T(8,128)S(1)} %fusion.102), channel_id=1, replica_groups=mesh['row'=8,'col'=4] {'row'}, use_global_device_ids=true, to_apply=%region_11.15 | all-reduce | flops 4096 | bytes 32768 | tf_op jit(solution)/shard_map/psum | solution.py:85
  584.5 5.8 cholesky.315
  591.7 4.9 custom-call.29
  597.7 1.1 copy.86
  599.4 8.3 %all-gather.3 = f32[8,96,64]{1,2,0:T(8,128)S(1)} all-gather(f32[1,96,64]{1,2,0:T(8,128)S(1)} %bitcast.267), channel_id=1, replica_groups=mesh['row'=8,'col'=4] {'row'}, dimensions={0}, use_global_device_ids=true | all-gather | bytes 221184 | tf_op jit(solution)/shard_map/all_gather | solution.py:87
  608.7 22.2 %reduce-scatter.11.cloned.1.call-done = f32[64,16,8]{0,1,2:T(8,128)} async-done(((f32[64,16,64]{0,1,2:T(8,128)}), f32[64,16,8]{0,1,2:T(8,128)}) %reduce-scatter.11.cloned.1.call-update) | async-done | bytes 32784 | tf_op jit(solution)/shard_map/reduce_scatter | solution.py:90
  (145 shorter events, 37.2 us)
Async XLA Ops:
  7.2 0.9 copy-start
  7.2 3.7 copy-start.6
  7.2 28.7 %reduce-scatter.5.cloned.1.call-start = ((), (), s32[]{:S(2)}) async-start(), calls=%async_computation.5 | async-start | bytes 327680 | tf_op jit(solution)/shard_map/reduce_scatter | solution.py:57
  12.1 35.1 %copy-start.1 = (f32[16,32,768]{2,1,0:T(8,128)S(1)}, f32[16,32,768]{2,1,0:T(8,128)}, u32[]{:S(2)}) copy-start(f32[16,32,768]{2,1,0:T(8,128)} %param.9) | copy-start | bytes 4718596
  13.0 75.0 %all-reduce.4.cloned.1.call-start = ((), (), s32[]{:S(2)}) async-start(), calls=%async_computation.6 | async-start | bytes 131072 | tf_op jit(solution)/shard_map/psum | solution.py:59
  59.9 3.8 copy-start.7
  59.9 131.4 %all-to-all-start = ((f32[8,1,49152]{2,1,0:T(1,128)}), f32[8,1,49152]{2,1,0:T(1,128)S(1)}, u32[]{:S(2)}, u32[]{:S(2)}) async-start(f32[8,1,49152]{2,1,0:T(1,128)} %reshape.61), calls=%async_computation.2 | async-start | bytes 3145728 | tf_op jit(solution)/shard_map/all_to_all | solution.py:70
  63.6 112.3 %reduce-scatter.7.cloned.1.call-start = ((), (), s32[]{:S(2)}) async-start(), calls=%async_computation.7 | async-start | bytes 589824 | tf_op jit(solution)/shard_map/reduce_scatter | solution.py:65
  88.0 41.2 %copy-start.4 = (f32[128,128]{1,0:T(8,128)S(1)}, f32[128,128]{1,0:T(8,128)}, u32[]{:S(2)}) copy-start(f32[128,128]{1,0:T(8,128)} %all-reduce.4.cloned.1.call-done) | copy-start | bytes 196612
  144.4 100.6 %all-reduce.6.cloned.1.call-start = ((), (), s32[]{:S(2)}) async-start(), calls=%async_computation.8 | async-start | bytes 131072 | tf_op jit(solution)/shard_map/psum | solution.py:67
  191.0 156.3 %reduce-scatter.9.cloned.1.call-start = ((), (), s32[]{:S(2)}) async-start(), calls=%async_computation.9 | async-start | bytes 2621440 | tf_op jit(solution)/shard_map/reduce_scatter | solution.py:76
  245.0 41.2 %copy-start.5 = (f32[128,128]{1,0:T(8,128)S(1)}, f32[128,128]{1,0:T(8,128)}, u32[]{:S(2)}) copy-start(f32[128,128]{1,0:T(8,128)} %all-reduce.6.cloned.1.call-done) | copy-start | bytes 196612
  304.1 76.8 %all-gather.6.cloned.1.call-start = ((), (), s32[]{:S(2)}) async-start(), calls=%async_computation.10 | async-start | bytes 3538944 | tf_op jit(solution)/shard_map/all_gather | solution.py:79
  347.3 33.6 %copy-start.2 = (f32[96,1024]{0,1:T(8,128)S(1)}, f32[96,1024]{0,1:T(8,128)}, u32[]{:S(2)}) copy-start(f32[96,1024]{0,1:T(8,128)} %reduce-scatter.9.cloned.1.call-done) | copy-start | bytes 1179652
  349.4 72.9 %all-reduce.8.cloned.1.call-start = ((), (), s32[]{:S(2)}) async-start(), calls=%async_computation.11 | async-start | bytes 589824 | tf_op jit(solution)/shard_map/psum | solution.py:80
  386.2 244.8 %reduce-scatter.11.cloned.1.call-start = ((), (), s32[]{:S(2)}) async-start(), calls=%async_computation.12 | async-start | bytes 589824 | tf_op jit(solution)/shard_map/reduce_scatter | solution.py:90
  422.3 46.0 %copy-start.3 = (f32[96,768]{1,0:T(8,128)S(1)}, f32[96,768]{1,0:T(8,128)}, u32[]{:S(2)}) copy-start(f32[96,768]{1,0:T(8,128)} %all-reduce.8.cloned.1.call-done) | copy-start | bytes 884740
Sparse Core Ops, SparseCore 0:
  13.2 22.7 reduce-scatter.4
  47.4 31.5 all-reduce.3
  144.5 31.4 reduce-scatter.6
  191.2 53.7 all-reduce.5
  304.3 43.0 reduce-scatter.8
  349.5 31.3 all-gather.5
  386.4 35.9 all-reduce.7
  598.9 32.0 reduce-scatter.10
where the time goes:
time: 644 us; the launch traced here: 638 us
  waiting for transfers between devices  205 us (32%)
  blocking collectives  190 us (30%)
  other arithmetic  151 us (23%)
  local copies, waits for them, and re-layouts  39.1 us (6%)
  matrix products  33.9 us (5%)
  between operations  15.1 us (2%)
    psum x4, blocking collectives, on_device(): inner = lax.psum(left_product(image, image), 'row')  93.5 us
    another operation x36, other arithmetic, orthonormal(): lower = jnp.linalg.cholesky(inner)  78.2 us
    another operation x24, other arithmetic, orthonormal(): return jax.scipy.linalg.solve_triangular(lower, matrix.T, lower=True).T  66.7 us
    reduce_scatter x1, waiting for transfers between devices, on_device(): lax.psum_scatter(part_three.reshape(cells_here, rank * rank), 'col', scat...  43.1 us
    psum x1, waiting for transfers between devices, on_device(): gram_three = lax.psum(gram_part_three, 'col')  35.4 us
    all_gather x4, blocking collectives, on_device(): basis_three = lax.all_gather(own_three, 'row', axis=0, tiled=True)  35.2 us
    all_gather x1, waiting for transfers between devices, on_device(): lax.all_gather(slab_three, 'row', axis=0, tiled=True)  31.5 us
    psum x1, waiting for transfers between devices, on_device(): gram_two = lax.psum(right_product(slab_rows_two, slab_rows_two), 'row')  31 us
  transfers between devices with their start and end apart: 9, of which 7 were waited for; matrix products, arithmetic and copies ran while one was open for 15% of the time, Pallas kernels for 0%

commit v1 on v0

--- a/solution.py
+++ b/solution.py
@@ -82,7 +82,9 @@
     own_three = start_three
     for iteration in range(STEPS):
         image = product(gram_three, basis_three)
-        inner = lax.psum(left_product(image, image), "row")
+        block = left_product(image, image)
+        shards = lax.all_gather(block, "row", axis=0, tiled=False)
+        inner = shards.sum(axis=0)
         own_three = orthonormal(image, inner)
         basis_three = lax.all_gather(own_three, "row", axis=0, tiled=True)
     core_part = left_product(own_three, slab_three)

time: 644 us -> 587 us (0.911)
  blocking collectives: 190 us -> 133 us
    psum x4 -> x0, blocking collectives: 93.5 us -> none  [on_device(): inner = lax.psum(left_product(image, image), 'row')]
    all_gather x0 -> x4, blocking collectives: none -> 34.5 us  [on_device(): shards = lax.all_gather(block, 'row', axis=0, tiled=False)]
  transfers between devices with their start and end apart: 9 -> 9, of which waited for: 7 -> 7; matrix products, arithmetic and copies ran while one was open for 15% -> 16% of each run, Pallas kernels for 0% -> 0%
where the time goes in v1:
time: 587 us; the launch traced here: 581 us
  waiting for transfers between devices  205 us (35%)
  other arithmetic  151 us (26%)
  blocking collectives  133 us (23%)
  local copies, waits for them, and re-layouts  39 us (7%)
  matrix products  33.9 us (6%)
  between operations  15.1 us (3%)
    another operation x36, other arithmetic, orthonormal(): lower = jnp.linalg.cholesky(inner)  78.2 us
    another operation x24, other arithmetic, orthonormal(): return jax.scipy.linalg.solve_triangular(lower, matrix.T, lower=True).T  66.7 us
    reduce_scatter x1, waiting for transfers between devices, on_device(): lax.psum_scatter(part_three.reshape(cells_here, rank * rank), 'col', scat...  43.1 us
    all_gather x4, blocking collectives, on_device(): basis_three = lax.all_gather(own_three, 'row', axis=0, tiled=True)  37 us
    psum x1, waiting for transfers between devices, on_device(): gram_three = lax.psum(gram_part_three, 'col')  35.4 us
    all_gather x4, blocking collectives, on_device(): shards = lax.all_gather(block, 'row', axis=0, tiled=False)  34.5 us
    all_gather x1, waiting for transfers between devices, on_device(): lax.all_gather(slab_three, 'row', axis=0, tiled=True)  31.5 us
    psum x1, waiting for transfers between devices, on_device(): gram_two = lax.psum(right_product(slab_rows_two, slab_rows_two), 'row')  31 us
  transfers between devices with their start and end apart: 9, of which 7 were waited for; matrix products, arithmetic and copies ran while one was open for 16% of the time, Pallas kernels for 0%

profile of v1, /device:TPU:0, one launch (start us, length us, event | category | flops | bytes accessed | tf_op | source)
XLA Modules:
  0.0 581.0 jit_solution(2219288831843532793)
XLA Ops:
  8.1 2.8 fusion.2
  13.1 22.8 %reduce-scatter.5.cloned.1.call-done = f32[16,1024]{1,0:T(8,128)} async-done(((f32[16,4096]{1,0:T(8,128)}), f32[16,1024]{1,0:T(8,128)}) %reduce-scatter.5.cloned.1.call-update) | async-done | bytes 65552 | tf_op jit(solution)/shard_map/reduce_scatter | solution.py:57
  35.9 10.1 %all_gather.51 = f32[128,1024]{1,0:T(8,128)S(1)} all-gather(f32[16,1024]{1,0:T(8,128)} %reduce-scatter.5.cloned.1.call-done), channel_id=1, replica_groups=mesh['row'=8,'col'=4] {'row'}, dimensions={0}, use_global_device_ids=true | all-gather | bytes 589824 | tf_op jit(solution)/shard_map/all_gather | solution.py:58
  46.0 1.2 fusion.76
  47.2 5.0 copy.59
  52.3 7.6 %reshape.65 = f32[8,1,49152]{2,1,0:T(1,128)} reshape(f32[768,16,32]{2,1,0:T(8,128)} %bitcast.266) | data formatting | bytes 3145728
  59.9 3.7 all-to-all-start
  63.7 24.3 %all_gather.52 = f32[128,64]{1,0:T(8,128)S(1)} all-gather(f32[16,64]{1,0:T(8,128)S(1)} %copy-done.7), channel_id=1, replica_groups=mesh['row'=8,'col'=4] {'row'}, dimensions={0}, use_global_device_ids=true | all-gather | bytes 36864 | tf_op jit(solution)/shard_map/all_gather | solution.py:60
  88.0 1.2 fusion.77
  89.5 5.8 %cholesky.194 = f32[64,64]{1,0:T(8,128)S(1)} custom-call(f32[64,64]{1,0:T(8,128)S(1)} %fusion.64), custom_call_target="Cholesky" | custom-call | tf_op jit(solution)/shard_map/jit(cholesky)/cholesky | solution.py:34
  96.7 4.9 custom-call.18
  103.2 5.8 %cholesky.205 = f32[64,64]{1,0:T(8,128)S(1)} custom-call(f32[64,64]{1,0:T(8,128)S(1)} %fusion.60), custom_call_target="Cholesky" | custom-call | tf_op jit(solution)/shard_map/jit(cholesky)/cholesky | solution.py:34
  110.4 4.9 custom-call.19
  115.5 1.1 fusion.81
  116.9 5.8 %cholesky.216 = f32[64,64]{1,0:T(8,128)S(1)} custom-call(f32[64,64]{1,0:T(8,128)S(1)} %fusion.56), custom_call_target="Cholesky" | custom-call | tf_op jit(solution)/shard_map/jit(cholesky)/cholesky | solution.py:34
  124.1 4.9 custom-call.20
  129.8 5.8 %cholesky.227 = f32[64,64]{1,0:T(8,128)S(1)} custom-call(f32[64,64]{1,0:T(8,128)S(1)} %fusion.52), custom_call_target="Cholesky" | custom-call | tf_op jit(solution)/shard_map/jit(cholesky)/cholesky | solution.py:34
  137.0 4.9 custom-call.21
  143.2 1.1 reshape.42
  144.4 13.1 %all_gather.54 = f32[128,64]{1,0:T(8,128)S(1)} all-gather(f32[32,64]{1,0:T(8,128)S(1)} %copy-done.6), channel_id=1, replica_groups=mesh['row'=8,'col'=4] {'col'}, dimensions={0}, use_global_device_ids=true | all-gather | bytes 40960 | tf_op jit(solution)/shard_map/all_gather | solution.py:68
  157.6 18.4 %reduce-scatter.7.cloned.1.call-done = f32[32,512]{1,0:T(8,128)} async-done(((f32[32,4096]{1,0:T(8,128)}), f32[32,512]{1,0:T(8,128)}) %reduce-scatter.7.cloned.1.call-update) | async-done | bytes 65552 | tf_op jit(solution)/shard_map/reduce_scatter | solution.py:65
  176.0 14.0 %all_gather.53 = f32[128,512]{1,0:T(8,128)S(1)} all-gather(f32[32,512]{1,0:T(8,128)} %reduce-scatter.7.cloned.1.call-done), channel_id=1, replica_groups=mesh['row'=8,'col'=4] {'col'}, dimensions={0}, use_global_device_ids=true | all-gather | bytes 327680 | tf_op jit(solution)/shard_map/all_gather | solution.py:66
  191.8 4.4 reduce.4
  196.2 4.7 reshape.66
  200.9 5.2 copy.60
  206.2 2.3 reshape.43
  208.5 1.9 copy.61
  210.4 3.5 fusion.29
  213.9 31.0 %all-reduce.6.cloned.1.call-done = f32[128,128]{1,0:T(8,128)} async-done(((f32[128,128]{1,0:T(8,128)}), f32[128,128]{1,0:T(8,128)}) %all-reduce.6.cloned.1.call-update) | async-done | bytes 65552 | tf_op jit(solution)/shard_map/psum | solution.py:67
  245.0 1.2 fusion.86
  246.4 5.8 %cholesky.238 = f32[64,64]{1,0:T(8,128)S(1)} custom-call(f32[64,64]{1,0:T(8,128)S(1)} %fusion.47), custom_call_target="Cholesky" | custom-call | tf_op jit(solution)/shard_map/jit(cholesky)/cholesky | solution.py:34
  253.6 4.9 custom-call.22
  260.1 5.8 %cholesky.249 = f32[64,64]{1,0:T(8,128)S(1)} custom-call(f32[64,64]{1,0:T(8,128)S(1)} %fusion.43), custom_call_target="Cholesky" | custom-call | tf_op jit(solution)/shard_map/jit(cholesky)/cholesky | solution.py:34
  267.3 4.9 custom-call.23
  273.9 5.8 %cholesky.260 = f32[64,64]{1,0:T(8,128)S(1)} custom-call(f32[64,64]{1,0:T(8,128)S(1)} %fusion.39), custom_call_target="Cholesky" | custom-call | tf_op jit(solution)/shard_map/jit(cholesky)/cholesky | solution.py:34
  281.0 4.9 custom-call.24
  286.7 5.8 %cholesky.271 = f32[64,64]{1,0:T(8,128)S(1)} custom-call(f32[64,64]{1,0:T(8,128)S(1)} %fusion.35), custom_call_target="Cholesky" | custom-call | tf_op jit(solution)/shard_map/jit(cholesky)/cholesky | solution.py:34
  293.9 5.0 custom-call.25
  299.2 2.3 convolution_bitcast_fusion
  301.5 2.6 copy.64
  304.2 43.1 %reduce-scatter.9.cloned.1.call-done = f32[96,1024]{0,1:T(8,128)} async-done(((f32[96,4096]{0,1:T(8,128)}), f32[96,1024]{0,1:T(8,128)}) %reduce-scatter.9.cloned.1.call-update) | async-done | bytes 393232 | tf_op jit(solution)/shard_map/reduce_scatter | solution.py:76
  347.3 2.0 copy.65
  349.4 31.5 %all-gather.10.cloned.1.call-done = f32[768,1024]{1,0:T(8,128)} async-done(((f32[96,1024]{1,0:T(8,128)}), f32[768,1024]{1,0:T(8,128)}) %all-gather.10.cloned.1.call-update) | async-done | bytes 3145744 | tf_op jit(solution)/shard_map/all_gather | solution.py:79
  380.9 5.3 fusion.94
  386.9 35.4 %all-reduce.8.cloned.1.call-done = f32[96,768]{1,0:T(8,128)} async-done(((f32[96,768]{1,0:T(8,128)}), f32[96,768]{1,0:T(8,128)}) %all-reduce.8.cloned.1.call-update) | async-done | bytes 294928 | tf_op jit(solution)/shard_map/psum | solution.py:80
  422.3 1.5 fusion.95
  424.0 9.3 %all-gather = f32[512,64]{1,0:T(8,128)S(1)} all-gather(f32[64,64]{1,0:T(8,128)S(1)} %fusion.96), channel_id=2, replica_groups=mesh['row'=8,'col'=4] {'row'}, dimensions={0}, use_global_device_ids=true | all-gather | bytes 147456 | tf_op jit(solution)/shard_map/all_gather | solution.py:86
  433.4 5.8 %cholesky.282 = f32[64,64]{1,0:T(8,128)S(1)} custom-call(f32[64,64]{1,0:T(8,128)S(1)} %fusion.28), custom_call_target="Cholesky" | custom-call | tf_op jit(solution)/shard_map/jit(cholesky)/cholesky | solution.py:34
  440.6 4.9 custom-call.26
  445.7 9.3 %all-gather.4 = f32[8,96,64]{1,2,0:T(8,128)S(1)} all-gather(f32[1,96,64]{1,2,0:T(8,128)S(1)} %convolution_bitcast_fusion.5), channel_id=1, replica_groups=mesh['row'=8,'col'=4] {'row'}, dimensions={0}, use_global_device_ids=true | all-gather | bytes 221184 | tf_op jit(solution)/shard_map/all_gather | solution.py:89
  455.9 8.6 %all-gather.1 = f32[512,64]{1,0:T(8,128)S(1)} all-gather(f32[64,64]{1,0:T(8,128)S(1)} %fusion.98), channel_id=3, replica_groups=mesh['row'=8,'col'=4] {'row'}, dimensions={0}, use_global_device_ids=true | all-gather | bytes 147456 | tf_op jit(solution)/shard_map/all_gather | solution.py:86
  464.6 5.8 %cholesky.293 = f32[64,64]{1,0:T(8,128)S(1)} custom-call(f32[64,64]{1,0:T(8,128)S(1)} %fusion.25), custom_call_target="Cholesky" | custom-call | tf_op jit(solution)/shard_map/jit(cholesky)/cholesky | solution.py:34
  471.8 4.9 custom-call.27
  476.9 9.3 %all-gather.5 = f32[8,96,64]{1,2,0:T(8,128)S(1)} all-gather(f32[1,96,64]{1,2,0:T(8,128)S(1)} %convolution_bitcast_fusion.4), channel_id=1, replica_groups=mesh['row'=8,'col'=4] {'row'}, dimensions={0}, use_global_device_ids=true | all-gather | bytes 221184 | tf_op jit(solution)/shard_map/all_gather | solution.py:89
  487.1 8.4 %all-gather.2 = f32[512,64]{1,0:T(8,128)S(1)} all-gather(f32[64,64]{1,0:T(8,128)S(1)} %fusion.100), channel_id=4, replica_groups=mesh['row'=8,'col'=4] {'row'}, dimensions={0}, use_global_device_ids=true | all-gather | bytes 147456 | tf_op jit(solution)/shard_map/all_gather | solution.py:86
  495.6 5.8 %cholesky.304 = f32[64,64]{1,0:T(8,128)S(1)} custom-call(f32[64,64]{1,0:T(8,128)S(1)} %fusion.22), custom_call_target="Cholesky" | custom-call | tf_op jit(solution)/shard_map/jit(cholesky)/cholesky | solution.py:34
  502.8 4.9 custom-call.28
  507.9 9.3 %all-gather.6 = f32[8,96,64]{1,2,0:T(8,128)S(1)} all-gather(f32[1,96,64]{1,2,0:T(8,128)S(1)} %convolution_bitcast_fusion.3), channel_id=1, replica_groups=mesh['row'=8,'col'=4] {'row'}, dimensions={0}, use_global_device_ids=true | all-gather | bytes 221184 | tf_op jit(solution)/shard_map/all_gather | solution.py:89
  518.1 8.4 %all-gather.3 = f32[512,64]{1,0:T(8,128)S(1)} all-gather(f32[64,64]{1,0:T(8,128)S(1)} %fusion.102), channel_id=5, replica_groups=mesh['row'=8,'col'=4] {'row'}, dimensions={0}, use_global_device_ids=true | all-gather | bytes 147456 | tf_op jit(solution)/shard_map/all_gather | solution.py:86
  526.6 5.8 %cholesky.315 = f32[64,64]{1,0:T(8,128)S(1)} custom-call(f32[64,64]{1,0:T(8,128)S(1)} %fusion.19), custom_call_target="Cholesky" | custom-call | tf_op jit(solution)/shard_map/jit(cholesky)/cholesky | solution.py:34
  533.7 4.9 custom-call.29
  539.7 1.1 copy.74
  541.5 9.2 %all-gather.7 = f32[8,96,64]{1,2,0:T(8,128)S(1)} all-gather(f32[1,96,64]{1,2,0:T(8,128)S(1)} %bitcast.275), channel_id=1, replica_groups=mesh['row'=8,'col'=4] {'row'}, dimensions={0}, use_global_device_ids=true | all-gather | bytes 221184 | tf_op jit(solution)/shard_map/all_gather | solution.py:89
  551.7 22.3 %reduce-scatter.11.cloned.1.call-done = f32[64,16,8]{0,1,2:T(8,128)} async-done(((f32[64,16,64]{0,1,2:T(8,128)}), f32[64,16,8]{0,1,2:T(8,128)}) %reduce-scatter.11.cloned.1.call-update) | async-done | bytes 32784 | tf_op jit(solution)/shard_map/reduce_scatter | solution.py:92
  (149 shorter events, 37.3 us)
Async XLA Ops:
  7.2 0.9 copy-start
  7.2 3.7 copy-start.6
  7.2 28.7 %reduce-scatter.5.cloned.1.call-start = ((), (), s32[]{:S(2)}) async-start(), calls=%async_computation.5 | async-start | bytes 327680 | tf_op jit(solution)/shard_map/reduce_scatter | solution.py:57
  12.1 35.1 %copy-start.1 = (f32[16,32,768]{2,1,0:T(8,128)S(1)}, f32[16,32,768]{2,1,0:T(8,128)}, u32[]{:S(2)}) copy-start(f32[16,32,768]{2,1,0:T(8,128)} %param.9) | copy-start | bytes 4718596
  13.0 75.0 %all-reduce.4.cloned.1.call-start = ((), (), s32[]{:S(2)}) async-start(), calls=%async_computation.6 | async-start | bytes 131072 | tf_op jit(solution)/shard_map/psum | solution.py:59
  59.9 3.8 copy-start.7
  59.9 131.4 %all-to-all-start = ((f32[8,1,49152]{2,1,0:T(1,128)}), f32[8,1,49152]{2,1,0:T(1,128)S(1)}, u32[]{:S(2)}, u32[]{:S(2)}) async-start(f32[8,1,49152]{2,1,0:T(1,128)} %reshape.65), calls=%async_computation.2 | async-start | bytes 3145728 | tf_op jit(solution)/shard_map/all_to_all | solution.py:70
  63.6 112.3 %reduce-scatter.7.cloned.1.call-start = ((), (), s32[]{:S(2)}) async-start(), calls=%async_computation.7 | async-start | bytes 589824 | tf_op jit(solution)/shard_map/reduce_scatter | solution.py:65
  88.0 41.2 %copy-start.4 = (f32[128,128]{1,0:T(8,128)S(1)}, f32[128,128]{1,0:T(8,128)}, u32[]{:S(2)}) copy-start(f32[128,128]{1,0:T(8,128)} %all-reduce.4.cloned.1.call-done) | copy-start | bytes 196612
  144.4 100.6 %all-reduce.6.cloned.1.call-start = ((), (), s32[]{:S(2)}) async-start(), calls=%async_computation.8 | async-start | bytes 131072 | tf_op jit(solution)/shard_map/psum | solution.py:67
  191.0 156.3 %reduce-scatter.9.cloned.1.call-start = ((), (), s32[]{:S(2)}) async-start(), calls=%async_computation.9 | async-start | bytes 2621440 | tf_op jit(solution)/shard_map/reduce_scatter | solution.py:76
  245.0 41.2 %copy-start.5 = (f32[128,128]{1,0:T(8,128)S(1)}, f32[128,128]{1,0:T(8,128)}, u32[]{:S(2)}) copy-start(f32[128,128]{1,0:T(8,128)} %all-reduce.6.cloned.1.call-done) | copy-start | bytes 196612
  304.1 76.8 %all-gather.10.cloned.1.call-start = ((), (), s32[]{:S(2)}) async-start(), calls=%async_computation.10 | async-start | bytes 3538944 | tf_op jit(solution)/shard_map/all_gather | solution.py:79
  347.3 33.6 %copy-start.2 = (f32[96,1024]{0,1:T(8,128)S(1)}, f32[96,1024]{0,1:T(8,128)}, u32[]{:S(2)}) copy-start(f32[96,1024]{0,1:T(8,128)} %reduce-scatter.9.cloned.1.call-done) | copy-start | bytes 1179652
  349.4 72.9 %all-reduce.8.cloned.1.call-start = ((), (), s32[]{:S(2)}) async-start(), calls=%async_computation.11 | async-start | bytes 589824 | tf_op jit(solution)/shard_map/psum | solution.py:80
  386.2 187.7 %reduce-scatter.11.cloned.1.call-start = ((), (), s32[]{:S(2)}) async-start(), calls=%async_computation.12 | async-start | bytes 589824 | tf_op jit(solution)/shard_map/reduce_scatter | solution.py:92
  422.3 32.9 %copy-start.3 = (f32[96,768]{1,0:T(8,128)S(1)}, f32[96,768]{1,0:T(8,128)}, u32[]{:S(2)}) copy-start(f32[96,768]{1,0:T(8,128)} %all-reduce.8.cloned.1.call-done) | copy-start | bytes 884740
Sparse Core Ops, SparseCore 0:
  13.2 22.7 reduce-scatter.4
  47.4 31.5 all-reduce.3
  144.5 31.4 reduce-scatter.6
  191.2 53.7 all-reduce.5
  304.3 43.0 reduce-scatter.8
  349.5 31.3 all-gather.9
  386.4 35.9 all-reduce.7
  541.0 32.9 reduce-scatter.10
